TPU v7x, 32 devices: a whole 2x2x4 slice. The times are simulated.
32 devices in a mesh: expert: 4 (over y, x), dp: 8 (over z, core).
Axes of the slice: x: 2, y: 2, z: 4, core: 2. Of those that a mesh axis runs over, the one named last changes fastest.
Arguments:
- gradient: bfloat16 [4, 8, 32, 4096], P('expert', 'dp'), may hold values from -6700 to 6700
- momentum: float32 [4, 32, 4096], P('expert'), may hold values from -4 to 4
- variance: bfloat16 [4, 32, 4096], P('expert'), may hold values from 0.0099487305 to 1
- worker_error: float32 [4, 8, 32, 4096], P('expert', 'dp'), may hold values from -6 to 6
- server_error: float32 [4, 32, 4096], P('expert', 'dp'), may hold values from -4 to 4
Outputs:
- new_momentum: float32 [4, 32, 4096], P('expert')
- adam_step: bfloat16 [4, 32, 4096], P('expert')
- new_worker_error: float32 [4, 8, 32, 4096], P('expert', 'dp')
- new_server_error: float32 [4, 32, 4096], P('expert', 'dp')
All inputs are finite; a program needn't handle non-finite values. Where the computation divides by a largest or mean magnitude, that divisor is 1e-20 or more.
Results may differ from a plain program's by a relative error of at most 0.011.
Values may be sent and summed in bfloat16 or wider, within the bound.
No kernel may reach another device: no remote copies, remote signals or barrier semaphores. Data moves between devices by JAX's collectives and lax.ppermute only.
A program may use at most 128 MiB of HBM per device.

v0:
```python
import jax
import jax.numpy as jnp
from jax import lax
from jax.sharding import PartitionSpec as P

beta_one = 0.9
rms_limit = 5.0
scale_eps = 1e-06
adam_eps = 1e-08


def compress(values):
    row_scale = jnp.mean(jnp.abs(values), axis=-1, keepdims=True).astype(jnp.bfloat16)
    row_code = jnp.clip(values / (row_scale.astype(jnp.float32) + scale_eps), -1.0, 1.0).astype(
        jnp.bfloat16
    )
    decoded = row_scale.astype(jnp.float32) * row_code.astype(jnp.float32)
    return (row_scale, row_code, decoded)


def per_device(gradient, momentum, variance, worker_error, server_error):
    grad_local = gradient[0, 0].astype(jnp.float32)
    squares = lax.psum(jnp.sum(jnp.square(grad_local)), "expert")
    entry_count = lax.axis_size("expert") * grad_local.shape[0] * grad_local.shape[1]
    root_mean = jnp.sqrt(squares / entry_count + 1e-06)
    clip_factor = jnp.minimum(1.0, rms_limit / root_mean)
    clipped = grad_local * clip_factor
    compensated = beta_one * momentum[0] + (1.0 - beta_one) * clipped + worker_error[0, 0]
    row_scale, row_code, decoded = compress(compensated)
    worker_new = compensated - decoded
    replicas = lax.axis_size("dp")
    group_rows = server_error.shape[1]
    codes_in, scales_in = (
        lax.all_to_all(row_code, "dp", split_axis=0, concat_axis=0, tiled=True),
        lax.all_to_all(row_scale, "dp", split_axis=0, concat_axis=0, tiled=True),
    )
    products = scales_in.astype(jnp.float32) * codes_in.astype(jnp.float32)
    average = jnp.sum(products.reshape(replicas, group_rows, products.shape[1]), axis=0) / replicas
    combined = average + server_error[0]
    owner_scale, owner_code, owner_decoded = compress(combined)
    server_new = combined - owner_decoded
    codes_all, scales_all = (
        lax.all_gather(owner_code, "dp", axis=0, tiled=True),
        lax.all_gather(owner_scale, "dp", axis=0, tiled=True),
    )
    momentum_new = scales_all.astype(jnp.float32) * codes_all.astype(jnp.float32)
    step_out = (momentum_new / (jnp.sqrt(variance[0].astype(jnp.float32)) + adam_eps)).astype(
        jnp.bfloat16
    )
    return (momentum_new[None], step_out[None], worker_new[None, None], server_new[None])


def solution(mesh):
    placed = (
        P("expert", "dp", None, None),
        P("expert", None, None),
        P("expert", None, None),
        P("expert", "dp", None, None),
        P("expert", "dp", None),
    )
    return jax.shard_map(
        per_device,
        mesh=mesh,
        in_specs=placed,
        out_specs=(
            P("expert", None, None),
            P("expert", None, None),
            P("expert", "dp", None, None),
            P("expert", "dp", None),
        ),
        check_vma=False,
    )
```

profile of v0, /device:TPU:0, one launch (start us, length us, event | category | flops | bytes accessed | tf_op | source)
XLA Modules:
  0.0 72.4 jit_solution(1911349935368470256)
XLA Ops:
  0.6 1.8 %fusion = f32[]{:T(128)} fusion(bf16[1,1,32,4096]{3,2,1,0:T(8,128)(2,1)} %param.5), kind=kLoop, calls=%fused_computation.2 | loop fusion | flops 393215 | bytes 262148 | tf_op jit(solution)/shard_map/reduce_sum | solution.py:23
  2.4 12.0 %psum.7 = f32[]{:T(128)} all-reduce(f32[]{:T(128)} %fusion), channel_id=1, replica_groups=mesh['expert'=4,'dp'=8] {'expert'}, use_global_device_ids=true, to_apply=%region_1.0 | all-reduce | flops 1 | bytes 8 | tf_op jit(solution)/shard_map/psum | solution.py:23
  15.1 1.5 %fusion.5 = f32[32]{0:T(128)S(1)} fusion(f32[1,1,32,4096]{3,2,1,0:T(8,128)} %param.8, f32[]{:T(128)S(6)} %min.27, bf16[1,1,32,4096]{3,2,1,0:T(8,128)(2,1)S(1)} %copy-done.2, f32[1,32,4096]{2,1,0:T(8,128)} %param.6), kind=kLoop, calls=%fused_computation.10 | loop fusion | flops 1048544 | bytes 1310852 | tf_op jit(solution)/shard_map/reduce_sum | solution.py:13
  16.6 0.7 convert_element_type.145
  17.3 4.9 %all-to-all-start = ((bf16[8,4,1]{1,2,0:T(2,128)(2,1)}), bf16[8,4,1]{1,2,0:T(2,128)(2,1)S(1)}, u32[]{:S(2)}, u32[]{:S(2)}) async-start(bf16[8,4,1]{1,2,0:T(2,128)(2,1)} %convert_element_type.145), calls=%async_computation | async-start | bytes 8192 | tf_op jit(solution)/shard_map/all_to_all | solution.py:35
  22.3 1.0 %copy-done = f32[1,1,32,4096]{3,2,1,0:T(8,128)S(1)} copy-done((f32[1,1,32,4096]{3,2,1,0:T(8,128)S(1)}, f32[1,1,32,4096]{3,2,1,0:T(8,128)}, u32[]{:S(2)}) %copy-start) | copy-done | bytes 524312
  23.2 0.1 squeeze.12
  23.5 1.0 %multiply_subtract_fusion = (f32[1,1,32,4096]{3,2,1,0:T(8,128)}, f32[1,1,32,4096]{3,2,1,0:T(8,128)S(1)}) fusion(f32[1,1,32,4096]{3,2,1,0:T(8,128)S(1)} %copy-done, f32[32]{0:T(128)S(1)} %get-tuple-element.12, f32[32]{0:T(128)S(1)} %get-tuple-element.11, f32[]{:T(128)S(6)} %min.27, bf16[1,1,32,4096]{3,2,1,0:T(8,128)(2,1)S(1)} %copy-done.2, ...), kind=kLoop, calls=%fused_computation.12 | loop fusion | flops 1572864 | bytes 2359556 | tf_op jit(solution)/shard_map/sub | solution.py:30
  24.4 0.1 mul.97
  24.6 0.1 mul.96
  24.7 1.0 %clamp_convert_fusion.1 = bf16[8,4,4096]{2,1,0:T(4,128)(2,1)} fusion(f32[8,4,4096]{2,1,0:T(4,128)S(1)} %squeeze.12, f32[8,4,4096]{2,1,0:T(4,128)S(1)} %mul.96, f32[8,4,4096]{2,1,0:T(4,128)S(1)} %mul.97, f32[8,4]{1,0:T(8,128)S(1)} %add.68), kind=kLoop, calls=%fused_computation.15 | loop fusion | flops 655360 | bytes 1835136 | tf_op jit(solution)/shard_map/convert_element_type | solution.py:14
  25.7 2.0 %all-to-all-done = bf16[8,4,1]{1,2,0:T(2,128)(2,1)S(1)} async-done(((bf16[8,4,1]{1,2,0:T(2,128)(2,1)}), bf16[8,4,1]{1,2,0:T(2,128)(2,1)S(1)}, u32[]{:S(2)}, u32[]{:S(2)}) %all-to-all-start) | async-done | bytes 96 | tf_op jit(solution)/shard_map/all_to_all | solution.py:35
  27.7 3.4 %all-to-all-start.1 = ((bf16[8,4,4096]{2,1,0:T(4,128)(2,1)}), bf16[8,4,4096]{2,1,0:T(4,128)(2,1)S(1)}, u32[]{:S(2)}, u32[]{:S(2)}) async-start(bf16[8,4,4096]{2,1,0:T(4,128)(2,1)} %clamp_convert_fusion.1), calls=%async_computation.1 | async-start | bytes 524288 | tf_op jit(solution)/shard_map/all_to_all | solution.py:34
  31.1 0.6 copy-done.5
  31.8 0.6 dynamic-slice
  33.0 0.1 copy.17
  33.2 7.5 %all-to-all-done.1 = bf16[8,4,4096]{2,1,0:T(4,128)(2,1)S(1)} async-done(((bf16[8,4,4096]{2,1,0:T(4,128)(2,1)}), bf16[8,4,4096]{2,1,0:T(4,128)(2,1)S(1)}, u32[]{:S(2)}, u32[]{:S(2)}) %all-to-all-start.1) | async-done | bytes 262176 | tf_op jit(solution)/shard_map/all_to_all | solution.py:34
  40.8 0.2 multiply_reduce_fusion
  41.0 0.1 abs_reduce_fusion
  41.2 14.2 %all-gather.1 = bf16[8,4,4096]{2,1,0:T(4,128)(2,1)S(1)} all-gather(bf16[1,4,4096]{2,1,0:T(4,128)(2,1)S(1)} %fusion.7), channel_id=1, replica_groups=mesh['expert'=4,'dp'=8] {'dp'}, dimensions={0}, use_global_device_ids=true | all-gather | bytes 294912 | tf_op jit(solution)/shard_map/all_gather | solution.py:43
  55.5 0.2 dynamic-update-slice
  55.7 14.8 %all-reduce = bf16[32]{0:T(256)(128)(2,1)S(1)} all-reduce(bf16[32]{0:T(256)(128)(2,1)S(1)} %dynamic-update-slice), channel_id=2, replica_groups=mesh['expert'=4,'dp'=8] {'dp'}, use_global_device_ids=true, to_apply=%add | all-reduce | flops 32 | bytes 128
  70.6 0.7 multiply_subtract_fusion.1
  71.3 1.1 %fusion.6 = (bf16[1,32,4096]{2,1,0:T(8,128)(2,1)}, f32[1,32,4096]{2,1,0:T(8,128)}) fusion(bf16[1,32,4096]{2,1,0:T(8,128)(2,1)S(1)} %copy-done.4, f32[32,4096]{1,0:T(8,128)S(1)} %reshape.172, f32[32]{0:T(128)S(1)} %mul.109), kind=kLoop, calls=%fused_computation.18 | loop fusion | flops 655360 | bytes 1572992 | tf_op jit(solution)/shard_map/broadcast_in_dim | solution.py:50
  (20 shorter events, 0.4 us)
Async XLA Ops:
  0.6 14.4 %copy-start.2 = (bf16[1,1,32,4096]{3,2,1,0:T(8,128)(2,1)S(1)}, bf16[1,1,32,4096]{3,2,1,0:T(8,128)(2,1)}, u32[]{:S(2)}) copy-start(bf16[1,1,32,4096]{3,2,1,0:T(8,128)(2,1)} %param.5) | copy-start | bytes 786436
  15.1 7.1 %copy-start.1 = (f32[1,32,4096]{2,1,0:T(8,128)S(1)}, f32[1,32,4096]{2,1,0:T(8,128)}, u32[]{:S(2)}) copy-start(f32[1,32,4096]{2,1,0:T(8,128)} %param.6) | copy-start | bytes 1572868
  17.3 10.4 %all-to-all-start = ((bf16[8,4,1]{1,2,0:T(2,128)(2,1)}), bf16[8,4,1]{1,2,0:T(2,128)(2,1)S(1)}, u32[]{:S(2)}, u32[]{:S(2)}) async-start(bf16[8,4,1]{1,2,0:T(2,128)(2,1)} %convert_element_type.145), calls=%async_computation | async-start | bytes 8192 | tf_op jit(solution)/shard_map/all_to_all | solution.py:35
  22.2 1.0 %copy-start = (f32[1,1,32,4096]{3,2,1,0:T(8,128)S(1)}, f32[1,1,32,4096]{3,2,1,0:T(8,128)}, u32[]{:S(2)}) copy-start(f32[1,1,32,4096]{3,2,1,0:T(8,128)} %param.8) | copy-start | bytes 1572868
  27.7 13.1 %all-to-all-start.1 = ((bf16[8,4,4096]{2,1,0:T(4,128)(2,1)}), bf16[8,4,4096]{2,1,0:T(4,128)(2,1)S(1)}, u32[]{:S(2)}, u32[]{:S(2)}) async-start(bf16[8,4,4096]{2,1,0:T(4,128)(2,1)} %clamp_convert_fusion.1), calls=%async_computation.1 | async-start | bytes 524288 | tf_op jit(solution)/shard_map/all_to_all | solution.py:34
  31.1 0.7 copy-start.5
  33.2 7.8 %copy-start.3 = (f32[1,4,4096]{2,1,0:T(4,128)S(1)}, f32[1,4,4096]{2,1,0:T(4,128)}, u32[]{:S(2)}) copy-start(f32[1,4,4096]{2,1,0:T(4,128)} %param.9) | copy-start | bytes 196612
  55.4 15.8 %copy-start.4 = (bf16[1,32,4096]{2,1,0:T(8,128)(2,1)S(1)}, bf16[1,32,4096]{2,1,0:T(8,128)(2,1)}, u32[]{:S(2)}) copy-start(bf16[1,32,4096]{2,1,0:T(8,128)(2,1)} %param.7) | copy-start | bytes 786436
where the time goes:
time: 72.8 us; the launch traced here: 72.4 us
  blocking collectives  41 us (56%)
  waiting for transfers between devices  9.54 us (13%)
  starting transfers between devices  8.29 us (11%)
  other arithmetic  7.52 us (10%)
  local copies, waits for them, and re-layouts  3.91 us (5%)
  between operations  2.09 us (3%)
    unnamed x1, blocking collectives  14.8 us
    all_gather x1, blocking collectives, per_device(): lax.all_gather(owner_code, 'dp', axis=0, tiled=True)  14.2 us
    psum x1, blocking collectives, per_device(): squares = lax.psum(jnp.sum(jnp.square(grad_local)), 'expert')  12 us
    all_to_all x1, waiting for transfers between devices, per_device(): lax.all_to_all(row_code, 'dp', split_axis=0, concat_axis=0, tiled=True)  7.55 us
    all_to_all x1, starting transfers between devices, per_device(): lax.all_to_all(row_scale, 'dp', split_axis=0, concat_axis=0, tiled=True)  4.88 us
    all_to_all x1, starting transfers between devices, per_device(): lax.all_to_all(row_code, 'dp', split_axis=0, concat_axis=0, tiled=True)  3.41 us
    unnamed x15, local copies, waits for them, and re-layouts  2.48 us
    all_to_all x1, waiting for transfers between devices, per_device(): lax.all_to_all(row_scale, 'dp', split_axis=0, concat_axis=0, tiled=True)  1.99 us
  transfers between devices with their start and end apart: 2, of which 2 were waited for; matrix products, arithmetic and copies ran while one was open for 5% of the time, Pallas kernels for 0%

commit v1 on v0

--- a/solution.py
+++ b/solution.py
@@ -1,3 +1,4 @@
+import functools
 import jax
 import jax.numpy as jnp
 from jax import lax
@@ -7,6 +8,39 @@
 rms_limit = 5.0
 scale_eps = 1e-06
 adam_eps = 1e-08
+
+
+def plan_groups_over_axis(x0, k_dim):
+    x0 = jnp.moveaxis(x0, 0, k_dim)
+    lower = x0.shape
+    current_block = x0.reshape(*lower[:k_dim], lower[k_dim] * lower[k_dim + 1], *lower[k_dim + 2 :])
+    return current_block
+
+
+def switch_yards(tile_in, row_axis):
+    after = lax.axis_size(row_axis)
+    carry_out = lax.axis_index(row_axis)
+    item_now, moved = (after, carry_out)
+    extra, mixed_arr = (tile_in[None], 1)
+    while mixed_arr < item_now:
+        view_out = lax.ppermute(
+            extra, axis_name=row_axis, perm=[(k, k ^ mixed_arr) for k in range(item_now)]
+        )
+        z1 = moved & mixed_arr == 0
+        carry_in = jnp.where(z1, extra, view_out)
+        earlier = jnp.where(z1, view_out, extra)
+        extra = jnp.concatenate([carry_in, earlier])
+        mixed_arr *= 2
+    return extra
+
+
+def change_the_clusters(sheet, my_data, dim_k):
+    h_now = switch_yards(sheet, my_data)
+    built = plan_groups_over_axis(h_now, dim_k)
+    return built
+
+
+digits_extend = functools.partial(change_the_clusters, my_data="dp", dim_k=0)
 
 
 def compress(values):
@@ -40,7 +74,7 @@
     owner_scale, owner_code, owner_decoded = compress(combined)
     server_new = combined - owner_decoded
     codes_all, scales_all = (
-        lax.all_gather(owner_code, "dp", axis=0, tiled=True),
+        digits_extend(owner_code),
         lax.all_gather(owner_scale, "dp", axis=0, tiled=True),
     )
     momentum_new = scales_all.astype(jnp.float32) * codes_all.astype(jnp.float32)

time: 72.8 us -> 67.7 us (0.930)
  blocking collectives: 41 us -> 26.9 us
  waiting for transfers between devices: 9.54 us -> 16.8 us
  local copies, waits for them, and re-layouts: 3.91 us -> 4.8 us
    all_gather x1 -> x0, blocking collectives: 14.2 us -> none  [per_device(): lax.all_gather(owner_code, 'dp', axis=0, tiled=True)]
    ppermute x0 -> x3, waiting for transfers between devices: none -> 5.4 us  [switch_yards(): lax.ppermute(extra, axis_name=row_axis, perm=[(k, k ^ mixed_arr) for k in...]
    all_to_all x1, waiting for transfers between devices: 7.55 us -> 9.44 us  [per_device(): lax.all_to_all(row_code, 'dp', split_axis=0, concat_axis=0, tiled=True)]
    convert_element_type x0 -> x3, other arithmetic: none -> 1.25 us  [the longest x1 1.08 us: per_device(): (momentum_new / (jnp.sqrt(variance[0].astype(jnp.float32)) + adam_eps)).a...]
    broadcast_in_dim x1 -> x0, other arithmetic: 1.09 us -> none  [per_device(): step_out[None]]
    unnamed x15, local copies, waits for them, and re-layouts: 2.48 us -> 3.23 us
  transfers between devices with their start and end apart: 2 -> 5, of which waited for: 2 -> 4; matrix products, arithmetic and copies ran while one was open for 5% -> 5% of each run, Pallas kernels for 0% -> 0%
where the time goes in v1:
time: 67.7 us; the launch traced here: 67.2 us
  blocking collectives  26.9 us (40%)
  waiting for transfers between devices  16.8 us (25%)
  starting transfers between devices  8.51 us (13%)
  other arithmetic  8 us (12%)
  local copies, waits for them, and re-layouts  4.8 us (7%)
  between operations  2.14 us (3%)
    unnamed x1, blocking collectives  14.9 us
    psum x1, blocking collectives, per_device(): squares = lax.psum(jnp.sum(jnp.square(grad_local)), 'expert')  12 us
    all_to_all x1, waiting for transfers between devices, per_device(): lax.all_to_all(row_code, 'dp', split_axis=0, concat_axis=0, tiled=True)  9.44 us
    ppermute x3, waiting for transfers between devices, switch_yards(): lax.ppermute(extra, axis_name=row_axis, perm=[(k, k ^ mixed_arr) for k in...  5.4 us
    all_to_all x1, starting transfers between devices, per_device(): lax.all_to_all(row_scale, 'dp', split_axis=0, concat_axis=0, tiled=True)  4.88 us
    all_to_all x1, starting transfers between devices, per_device(): lax.all_to_all(row_code, 'dp', split_axis=0, concat_axis=0, tiled=True)  3.41 us
    unnamed x15, local copies, waits for them, and re-layouts  3.23 us
    all_to_all x1, waiting for transfers between devices, per_device(): lax.all_to_all(row_scale, 'dp', split_axis=0, concat_axis=0, tiled=True)  1.99 us
  transfers between devices with their start and end apart: 5, of which 4 were waited for; matrix products, arithmetic and copies ran while one was open for 5% of the time, Pallas kernels for 0%

profile of v1, /device:TPU:0, one launch (start us, length us, event | category | flops | bytes accessed | tf_op | source)
XLA Modules:
  0.0 67.2 jit_solution(12784725359980112923)
XLA Ops:
  0.6 1.8 %fusion = f32[]{:T(128)} fusion(bf16[1,1,32,4096]{3,2,1,0:T(8,128)(2,1)} %param.5), kind=kLoop, calls=%fused_computation.2 | loop fusion | flops 393215 | bytes 262148 | tf_op jit(solution)/shard_map/reduce_sum | solution.py:57
  2.4 12.0 %psum.7 = f32[]{:T(128)} all-reduce(f32[]{:T(128)} %fusion), channel_id=1, replica_groups=mesh['expert'=4,'dp'=8] {'expert'}, use_global_device_ids=true, to_apply=%region_1.0 | all-reduce | flops 1 | bytes 8 | tf_op jit(solution)/shard_map/psum | solution.py:57
  15.1 1.5 %fusion.4 = f32[32]{0:T(128)S(1)} fusion(f32[1,1,32,4096]{3,2,1,0:T(8,128)} %param.8, f32[]{:T(128)S(6)} %min.23, bf16[1,1,32,4096]{3,2,1,0:T(8,128)(2,1)S(1)} %copy-done.2, f32[1,32,4096]{2,1,0:T(8,128)} %param.6), kind=kLoop, calls=%fused_computation.8 | loop fusion | flops 1048544 | bytes 1310852 | tf_op jit(solution)/shard_map/reduce_sum | solution.py:47
  16.6 0.7 %convert_element_type.156 = bf16[8,4,1]{1,2,0:T(2,128)(2,1)} reshape(bf16[32]{0:T(256)(128)(2,1)S(1)} %get-tuple-element.18) | data formatting | bytes 128 | tf_op jit(solution)/shard_map/convert_element_type | solution.py:47
  17.3 4.9 %all-to-all-start = ((bf16[8,4,1]{1,2,0:T(2,128)(2,1)}), bf16[8,4,1]{1,2,0:T(2,128)(2,1)S(1)}, u32[]{:S(2)}, u32[]{:S(2)}) async-start(bf16[8,4,1]{1,2,0:T(2,128)(2,1)} %convert_element_type.156), calls=%async_computation | async-start | bytes 8192 | tf_op jit(solution)/shard_map/all_to_all | solution.py:69
  22.3 1.0 %copy-done = f32[1,1,32,4096]{3,2,1,0:T(8,128)S(1)} copy-done((f32[1,1,32,4096]{3,2,1,0:T(8,128)S(1)}, f32[1,1,32,4096]{3,2,1,0:T(8,128)}, u32[]{:S(2)}) %copy-start) | copy-done | bytes 524312
  23.5 1.0 %multiply_subtract_fusion = (f32[1,1,32,4096]{3,2,1,0:T(8,128)}, f32[1,1,32,4096]{3,2,1,0:T(8,128)S(1)}) fusion(f32[1,1,32,4096]{3,2,1,0:T(8,128)S(1)} %copy-done, f32[32]{0:T(128)S(1)} %get-tuple-element.17, f32[32]{0:T(128)S(1)} %get-tuple-element.16, f32[]{:T(128)S(6)} %min.23, bf16[1,1,32,4096]{3,2,1,0:T(8,128)(2,1)S(1)} %copy-done.2, ...), kind=kLoop, calls=%fused_computation.10 | loop fusion | flops 1572864 | bytes 2359556 | tf_op jit(solution)/shard_map/sub | solution.py:64
  24.7 1.0 %clamp_convert_fusion.1 = bf16[8,4,4096]{2,1,0:T(4,128)(2,1)} fusion(f32[8,4,4096]{2,1,0:T(4,128)S(1)} %squeeze.12, f32[8,4,4096]{2,1,0:T(4,128)S(1)} %mul.103, f32[8,4,4096]{2,1,0:T(4,128)S(1)} %mul.104, f32[8,4]{1,0:T(8,128)S(1)} %add.67), kind=kLoop, calls=%fused_computation.14 | loop fusion | flops 655360 | bytes 1835136 | tf_op jit(solution)/shard_map/convert_element_type | solution.py:48
  25.7 2.0 %all-to-all-done = bf16[8,4,1]{1,2,0:T(2,128)(2,1)S(1)} async-done(((bf16[8,4,1]{1,2,0:T(2,128)(2,1)}), bf16[8,4,1]{1,2,0:T(2,128)(2,1)S(1)}, u32[]{:S(2)}, u32[]{:S(2)}) %all-to-all-start) | async-done | bytes 96 | tf_op jit(solution)/shard_map/all_to_all | solution.py:69
  27.7 3.4 %all-to-all-start.1 = ((bf16[8,4,4096]{2,1,0:T(4,128)(2,1)}), bf16[8,4,4096]{2,1,0:T(4,128)(2,1)S(1)}, u32[]{:S(2)}, u32[]{:S(2)}) async-start(bf16[8,4,4096]{2,1,0:T(4,128)(2,1)} %clamp_convert_fusion.1), calls=%async_computation.1 | async-start | bytes 524288 | tf_op jit(solution)/shard_map/all_to_all | solution.py:68
  31.3 9.4 %all-to-all-done.1 = bf16[8,4,4096]{2,1,0:T(4,128)(2,1)S(1)} async-done(((bf16[8,4,4096]{2,1,0:T(4,128)(2,1)}), bf16[8,4,4096]{2,1,0:T(4,128)(2,1)S(1)}, u32[]{:S(2)}, u32[]{:S(2)}) %all-to-all-start.1) | async-done | bytes 262176 | tf_op jit(solution)/shard_map/all_to_all | solution.py:68
  40.8 0.2 multiply_reduce_fusion
  41.0 0.1 fusion.6
  41.1 0.7 %multiply_subtract_fusion.1 = (f32[1,4,4096]{2,1,0:T(4,128)}, bf16[1,4,4096]{2,1,0:T(4,128)(2,1)S(1)}) fusion(f32[4]{0:T(128)S(1)} %get-tuple-element.20, f32[1,4,4096]{2,1,0:T(4,128)S(1)} %copy-done.3, f32[4,4096]{1,0:T(4,128)S(1)} %multiply_reduce_fusion, f32[4]{0:T(128)S(1)} %get-tuple-element.21), kind=kLoop, calls=%fused_computation.26 | loop fusion | flops 131072 | bytes 229408 | tf_op jit(solution)/shard_map/sub | solution.py:75
  41.9 1.2 %collective-permute-done = bf16[1,4,4096]{2,1,0:T(4,128)(2,1)S(1)} collective-permute-done((bf16[1,4,4096]{2,1,0:T(4,128)(2,1)S(1)}, bf16[1,4,4096]{2,1,0:T(4,128)(2,1)S(1)}, u32[]{:S(2)}, u32[]{:S(2)}) %collective-permute-start) | collective-permute-done | bytes 32800 | tf_op jit(solution)/shard_map/ppermute | solution.py:26
  43.3 4.2 %collective-permute-done.1 = bf16[2,4,4096]{2,1,0:T(4,128)(2,1)S(1)} collective-permute-done((bf16[2,4,4096]{2,1,0:T(4,128)(2,1)S(1)}, bf16[2,4,4096]{2,1,0:T(4,128)(2,1)S(1)}, u32[]{:S(2)}, u32[]{:S(2)}) %collective-permute-start.1) | collective-permute-done | bytes 65568 | tf_op jit(solution)/shard_map/ppermute | solution.py:26
  47.8 0.6 copy-done.5
  48.4 0.6 dynamic-slice
  49.7 0.2 dynamic-update-slice
  49.9 14.9 %all-reduce = bf16[32]{0:T(256)(128)(2,1)S(1)} all-reduce(bf16[32]{0:T(256)(128)(2,1)S(1)} %dynamic-update-slice), channel_id=2, replica_groups=mesh['expert'=4,'dp'=8] {'dp'}, use_global_device_ids=true, to_apply=%add | all-reduce | flops 32 | bytes 128
  65.0 0.2 maximum_convert_fusion
  65.2 0.2 reshape.221
  65.4 0.8 %copy-done.4 = bf16[1,32,4096]{2,1,0:T(8,128)(2,1)S(1)} copy-done((bf16[1,32,4096]{2,1,0:T(8,128)(2,1)S(1)}, bf16[1,32,4096]{2,1,0:T(8,128)(2,1)}, u32[]{:S(2)}) %copy-start.4) | copy-done | bytes 262168
  66.1 1.1 %divide_convert_fusion = (bf16[1,32,4096]{2,1,0:T(8,128)(2,1)}, f32[1,32,4096]{2,1,0:T(8,128)}) fusion(bf16[1,32,4096]{2,1,0:T(8,128)(2,1)S(1)} %copy-done.4, f32[1,32,4096]{2,1,0:T(8,128)S(1)} %reshape.221, f32[32]{0:T(128)S(1)} %mul.116), kind=kLoop, calls=%fused_computation.12 | loop fusion | flops 655360 | bytes 1572992 | tf_op jit(solution)/shard_map/convert_element_type | solution.py:81
  (30 shorter events, 1.4 us)
Async XLA Ops:
  0.6 14.4 %copy-start.2 = (bf16[1,1,32,4096]{3,2,1,0:T(8,128)(2,1)S(1)}, bf16[1,1,32,4096]{3,2,1,0:T(8,128)(2,1)}, u32[]{:S(2)}) copy-start(bf16[1,1,32,4096]{3,2,1,0:T(8,128)(2,1)} %param.5) | copy-start | bytes 786436
  15.1 7.1 %copy-start.1 = (f32[1,32,4096]{2,1,0:T(8,128)S(1)}, f32[1,32,4096]{2,1,0:T(8,128)}, u32[]{:S(2)}) copy-start(f32[1,32,4096]{2,1,0:T(8,128)} %param.6) | copy-start | bytes 1572868
  17.3 10.4 %all-to-all-start = ((bf16[8,4,1]{1,2,0:T(2,128)(2,1)}), bf16[8,4,1]{1,2,0:T(2,128)(2,1)S(1)}, u32[]{:S(2)}, u32[]{:S(2)}) async-start(bf16[8,4,1]{1,2,0:T(2,128)(2,1)} %convert_element_type.156), calls=%async_computation | async-start | bytes 8192 | tf_op jit(solution)/shard_map/all_to_all | solution.py:69
  22.2 1.0 %copy-start = (f32[1,1,32,4096]{3,2,1,0:T(8,128)S(1)}, f32[1,1,32,4096]{3,2,1,0:T(8,128)}, u32[]{:S(2)}) copy-start(f32[1,1,32,4096]{3,2,1,0:T(8,128)} %param.8) | copy-start | bytes 1572868
  27.7 13.1 %all-to-all-start.1 = ((bf16[8,4,4096]{2,1,0:T(4,128)(2,1)}), bf16[8,4,4096]{2,1,0:T(4,128)(2,1)S(1)}, u32[]{:S(2)}, u32[]{:S(2)}) async-start(bf16[8,4,4096]{2,1,0:T(4,128)(2,1)} %clamp_convert_fusion.1), calls=%async_computation.1 | async-start | bytes 524288 | tf_op jit(solution)/shard_map/all_to_all | solution.py:68
  31.3 9.7 %copy-start.3 = (f32[1,4,4096]{2,1,0:T(4,128)S(1)}, f32[1,4,4096]{2,1,0:T(4,128)}, u32[]{:S(2)}) copy-start(f32[1,4,4096]{2,1,0:T(4,128)} %param.9) | copy-start | bytes 196612
  41.9 1.2 %collective-permute-start = (bf16[1,4,4096]{2,1,0:T(4,128)(2,1)S(1)}, bf16[1,4,4096]{2,1,0:T(4,128)(2,1)S(1)}, u32[]{:S(2)}, u32[]{:S(2)}) collective-permute-start(bf16[1,4,4096]{2,1,0:T(4,128)(2,1)S(1)} %get-tuple-element.5), channel_id=1, source_target_pairs={{0,1},{1,0},{2,3},{3,2},{4,5},{5,4},{6,7},{7,6},{8,9},{9,8},{10,11... | collective-permute-start | bytes 98312 | tf_op jit(solution)/shard_map/ppermute | solution.py:26
  43.2 4.3 %collective-permute-start.1 = (bf16[2,4,4096]{2,1,0:T(4,128)(2,1)S(1)}, bf16[2,4,4096]{2,1,0:T(4,128)(2,1)S(1)}, u32[]{:S(2)}, u32[]{:S(2)}) collective-permute-start(bf16[2,4,4096]{2,1,0:T(4,128)(2,1)S(1)} %pad_maximum_fusion.1), channel_id=1, source_target_pairs={{0,2},{1,3},{2,0},{3,1},{4,6},{5,7},{6,4},{7,5},{8,10},{9,11},{10,... | collective-permute-start | bytes 196616 | tf_op jit(solution)/shard_map/ppermute | solution.py:26
  47.7 17.2 %collective-permute-start.2 = (bf16[4,4,4096]{2,1,0:T(4,128)(2,1)S(1)}, bf16[4,4,4096]{2,1,0:T(4,128)(2,1)S(1)}, u32[]{:S(2)}, u32[]{:S(2)}) collective-permute-start(bf16[4,4,4096]{2,1,0:T(4,128)(2,1)S(1)} %pad_maximum_fusion), channel_id=1, source_target_pairs={{0,4},{1,5},{2,6},{3,7},{4,0},{5,1},{6,2},{7,3},{8,12},{9,13},{10,... | collective-permute-start | bytes 393224 | tf_op jit(solution)/shard_map/ppermute | solution.py:26
  47.7 0.7 copy-start.5
  65.2 1.0 %copy-start.4 = (bf16[1,32,4096]{2,1,0:T(8,128)(2,1)S(1)}, bf16[1,32,4096]{2,1,0:T(8,128)(2,1)}, u32[]{:S(2)}) copy-start(bf16[1,32,4096]{2,1,0:T(8,128)(2,1)} %param.7) | copy-start | bytes 786436
